TPU v7x, 256 devices: a whole 4x4x8 slice. The times are simulated.
256 devices in a mesh: worker: 8 (over z_lo, core), fsdp: 32 (over x, y, z_hi).
Axes of the slice: x: 4, y: 4, z: 8 (z_hi: 2, z_lo: 4; z = z_hi * 4 + z_lo), core: 2. Of those that a mesh axis runs over, the one named last changes fastest.
Arguments:
- features: bfloat16 [49152, 8192], P(('worker', 'fsdp')), may hold values from -24 to 24
- value_cotangent: bfloat16 [49152, 512], P(('worker', 'fsdp')), may hold values from -6 to 6
- value_weight: float32 [8, 8192, 512], P('worker', 'fsdp'), may hold values from -0.25 to 0.25
- first_moment: float32 [8, 8192, 512], P('worker', 'fsdp'), may hold values from -48 to 48
- second_moment: float32 [8, 8192, 512], P('worker', 'fsdp'), may hold values from 1000 to 10000
- fragment_local: float32 [8, 8192, 512], P('worker', 'fsdp'), may hold values from -6 to 6
- fragment_anchor: float32 [8192, 512], P('fsdp'), may hold values from -6 to 6
- outer_momentum: float32 [8192, 512], P('fsdp'), may hold values from -3 to 3
Outputs:
- feature_grad: float32 [49152, 8192], P(('worker', 'fsdp'))
- new_weight: float32 [8, 8192, 512], P('worker', 'fsdp')
- new_first: float32 [8, 8192, 512], P('worker', 'fsdp')
- new_second: float32 [8, 8192, 512], P('worker', 'fsdp')
- new_anchor: float32 [8192, 512], P('fsdp')
- new_momentum: float32 [8192, 512], P('fsdp')
All inputs are finite; a program needn't handle non-finite values.
Results may differ from a plain program's by a relative error of at most 0.0003.
Values may be sent and summed in bfloat16 or wider, within the bound.
A program may use at most 128 MiB of HBM per device.

v0:
```python
import jax
import jax.numpy as jnp
from jax import lax
from jax.sharding import PartitionSpec as P

first_decay = 0.9
second_decay = 0.95
inner_rate = 0.001
weight_decay = 0.1
adam_epsilon = 1e-08
adam_count = 10.0
outer_rate = 0.7
outer_mass = 0.9


def on_device(
    features,
    value_cotangent,
    value_weight,
    first_moment,
    second_moment,
    fragment_local,
    fragment_anchor,
    outer_momentum,
):
    weight = value_weight[0]
    wide_cot = value_cotangent.astype(jnp.float32)
    feature_grad = jnp.dot(
        wide_cot,
        lax.all_gather(weight, "fsdp", axis=0, tiled=True).T,
        preferred_element_type=jnp.float32,
        precision=lax.Precision.HIGHEST,
    )
    gradient = lax.psum_scatter(
        lax.dot_general(
            features, value_cotangent, (((0,), (0,)), ((), ())), preferred_element_type=jnp.float32
        ),
        "fsdp",
        scatter_dimension=0,
        tiled=True,
    )
    first_new = first_decay * first_moment[0] + (1.0 - first_decay) * gradient
    second_new = second_decay * second_moment[0] + (1.0 - second_decay) * gradient * gradient
    first_hat = first_new / (1.0 - first_decay**adam_count)
    second_hat = second_new / (1.0 - second_decay**adam_count)
    weight_new = weight - inner_rate * (
        first_hat / (jnp.sqrt(second_hat) + adam_epsilon) + weight_decay * weight
    )
    workers = lax.axis_size("worker")
    pseudo_sum = lax.psum(fragment_anchor - fragment_local[0], "worker")
    pseudo_mean = pseudo_sum / workers
    new_momentum = outer_mass * outer_momentum + pseudo_mean
    new_anchor = fragment_anchor - outer_rate * (pseudo_mean + outer_mass * new_momentum)
    return (
        feature_grad,
        weight_new[None],
        first_new[None],
        second_new[None],
        new_anchor,
        new_momentum,
    )


def solution(mesh):
    placed = (
        P(("worker", "fsdp"), None),
        P(("worker", "fsdp"), None),
        P("worker", "fsdp", None),
        P("worker", "fsdp", None),
        P("worker", "fsdp", None),
        P("worker", "fsdp", None),
        P("fsdp", None),
        P("fsdp", None),
    )
    return jax.shard_map(
        on_device,
        mesh=mesh,
        in_specs=placed,
        out_specs=(
            P(("worker", "fsdp"), None),
            P("worker", "fsdp", None),
            P("worker", "fsdp", None),
            P("worker", "fsdp", None),
            P("fsdp", None),
            P("fsdp", None),
        ),
        check_vma=False,
    )
```

profile of v0, /device:TPU:32, one launch (start us, length us, event | category | flops | bytes accessed | tf_op | source)
XLA Modules:
  0.0 987.9 jit_solution(5719702654336958174)
XLA Ops:
  8.0 0.0 copy-start
  8.0 0.0 all-reduce.2.cloned.1.call-start
  8.1 2.2 bitcast_subtract_fusion
  10.3 0.0 all-reduce.2.cloned.1.call-update
  10.3 0.0 all-gather.3.cloned.1.call-start
  10.4 0.5 all-gather.3.cloned.1.call-update
  10.9 0.0 copy-start.1
  10.9 0.0 reduce-scatter.2.cloned.1.call-start
  10.9 0.0 copy-done
  11.0 9.1 fusion.8
  20.0 0.0 reduce-scatter.2.cloned.1.call-update
  20.1 88.5 %all-reduce.2.cloned.1.call-done = f32[256,512]{1,0:T(8,128)} async-done(((f32[256,512]{1,0:T(8,128)}), f32[256,512]{1,0:T(8,128)}) %all-reduce.2.cloned.1.call-update) | async-done | bytes 524304 | tf_op jit(solution)/shard_map/psum | solution.py:50
  108.6 2.5 multiply_subtract_fusion
  111.1 150.3 %all-gather.3.cloned.1.call-done = f32[1,8192,512]{2,1,0:T(8,128)} async-done(((f32[1,256,512]{2,1,0:T(8,128)}), f32[1,8192,512]{2,1,0:T(8,128)}) %all-gather.3.cloned.1.call-update) | async-done | bytes 16777232 | tf_op jit(solution)/shard_map/all_gather | solution.py:30
  261.4 0.0 copy-done.1
  261.4 16.2 %fusion = f32[192,8192]{1,0:T(8,128)} fusion(bf16[192,512]{1,0:T(8,128)(2,1)S(1)} %copy-done.1, f32[1,8192,512]{2,1,0:T(8,128)} %all-gather.3.cloned.1.call-done), kind=kOutput, calls=%fused_computation | convolution fusion | flops 9663676416 | bytes 23265280 | tf_op jit(solution)/shard_map/dot_general | solution.py:28
  277.5 699.9 %reduce-scatter.2.cloned.1.call-done = f32[256,512]{1,0:T(8,128)} async-done(((f32[8192,512]{1,0:T(8,128)}), f32[256,512]{1,0:T(8,128)}) %reduce-scatter.2.cloned.1.call-update) | async-done | bytes 524304 | tf_op jit(solution)/shard_map/reduce_scatter | solution.py:34
  977.4 3.0 fusion.7
Async XLA Ops:
  8.0 3.0 copy-start
  8.0 100.6 %all-reduce.2.cloned.1.call-start = ((), (), s32[]{:S(2)}) async-start(), calls=%async_computation.2 | async-start | bytes 1048576 | tf_op jit(solution)/shard_map/psum | solution.py:50
  10.3 251.1 %all-gather.3.cloned.1.call-start = ((), (), s32[]{:S(2)}) async-start(), calls=%async_computation.3 | async-start | bytes 17301504 | tf_op jit(solution)/shard_map/all_gather | solution.py:30
  10.9 250.5 %copy-start.1 = (bf16[192,512]{1,0:T(8,128)(2,1)S(1)}, bf16[192,512]{1,0:T(8,128)(2,1)}, u32[]{:S(2)}) copy-start(bf16[192,512]{1,0:T(8,128)(2,1)} %param.9) | copy-start | bytes 589828
  10.9 966.5 %reduce-scatter.2.cloned.1.call-start = ((), (), s32[]{:S(2)}) async-start(), calls=%async_computation.1 | async-start | bytes 17301504 | tf_op jit(solution)/shard_map/reduce_scatter | solution.py:34
Sparse Core Ops, SparseCore 0:
  12.1 96.4 all-reduce.1
Sparse Core Ops, SparseCore 1:
  14.2 247.1 all-gather.2
  263.8 713.6 reduce-scatter.1
where the time goes:
time: 993 us; the launch traced here: 988 us
  waiting for transfers between devices  939 us (95%)
  matrix products  25.3 us (3%)
  between operations  15.5 us (2%)
    reduce_scatter x1, waiting for transfers between devices, on_device(): lax.psum_scatter(lax.dot_general(features, value_cotangent, (((0,), (0,))...  700 us
    all_gather x1, waiting for transfers between devices, on_device(): lax.all_gather(weight, 'fsdp', axis=0, tiled=True)  150 us
    psum x1, waiting for transfers between devices, on_device(): pseudo_sum = lax.psum(fragment_anchor - fragment_local[0], 'worker')  88.5 us
  transfers between devices with their start and end apart: 3, of which 3 were waited for; matrix products, arithmetic and copies ran while one was open for 3% of the time, Pallas kernels for 0%

commit v1 on v0

v1 whole, which is shorter than its diff:
```python
import jax
import jax.numpy as jnp
from jax import lax
from jax.experimental import pallas as pl
from jax.experimental.pallas import tpu as pltpu
from jax.sharding import PartitionSpec as P

MESH = pl.DeviceIdType.MESH
F32 = jnp.float32
BF16 = jnp.bfloat16

first_decay = 0.9
second_decay = 0.95
inner_rate = 0.001
weight_decay = 0.1
adam_epsilon = 1e-08
adam_count = 10.0
outer_rate = 0.7
outer_mass = 0.9

RING = 4
TOK = 192
ROWS = 256
COLS = 512
WORKERS = 8
PART = ROWS // WORKERS

_count = 0


def _take(n):
    global _count
    base = _count
    _count += n
    return base


S_FEAT = _take(2 * 3 * RING)
S_COT1 = _take(4)
S_COT2 = _take(4)
S_WZ = _take(1)
S_W1 = _take(4)
S_W2 = _take(4)
S_R1 = _take(4)
S_R2 = _take(4)
S_GZ = _take(1)
S_OUT = _take(2 * 3 * RING)
S_LOC = _take(WORKERS - 1)
S_PSE = _take(WORKERS - 1)
N_REMOTE = _count

L_FEAT = 0
L_COT = 8
L_W = 10
L_IN = 11
L_OUT = 17
L_RES = 25
N_LOCAL = 30


def kernel(
    f_ref, c_ref, w_ref, fm_ref, sm_ref, fl_ref, fa_ref, om_ref,
    fg_ref, nw_ref, nf_ref, ns_ref, na_ref, nm_ref,
    fb, cb, wb, gb, rh, rf, zr, ob, wv, fmv, smv, fav, omv, fr, ps,
    nwv, nfv, nsv, nav, nmv,
    ssem, rsem, lsem,
):
    worker = lax.axis_index("worker")
    place = lax.axis_index("fsdp")
    x, y, zh = place // 8, (place // 2) % RING, place % 2

    zo = (zh, 1 - zh)
    gat = tuple(x * (1 - z) + y * z for z in zo)
    exc = tuple(y * (1 - z) + x * z for z in zo)

    def along_gather(o, d):
        z = zo[o]
        xx, yy = (x + d * (1 - z)) % RING, (y + d * z) % RING
        return (worker, (xx * RING + yy) * 2 + zh)

    def along_exchange(o, d):
        z = zo[o]
        xx, yy = (x + d * z) % RING, (y + d * (1 - z)) % RING
        return (worker, (xx * RING + yy) * 2 + zh)

    partner = (worker, place + 1 - 2 * zh)

    def other_worker(j):
        return ((worker + j) % WORKERS, place)

    def column(o, g, e):
        z = zo[o]
        start = g * (2048 - 1536 * z) + e * (512 + 1536 * z) + z * ROWS
        return pl.ds(pl.multiple_of(start, ROWS), ROWS)

    def tokens(e, half=None):
        if half is None:
            return pl.ds(pl.multiple_of(e * TOK, 16), TOK)
        return pl.ds(pl.multiple_of(e * TOK + half * (TOK // 2), 16), TOK // 2)

    sent = []

    def send(src, dst, sem, device):
        copy = pltpu.make_async_remote_copy(
            src_ref=src, dst_ref=dst, send_sem=ssem.at[sem], recv_sem=rsem.at[sem],
            device_id=device, device_id_type=MESH,
        )
        copy.start()
        sent.append(copy)
        return copy

    def local(src, dst, sem):
        copy = pltpu.make_async_copy(src, dst, lsem.at[sem])
        copy.start()
        return copy

    barrier = pltpu.get_barrier_semaphore()
    peers = [along_gather(0, d) for d in (1, 2, 3)] + [along_exchange(0, d) for d in (1, 2, 3)]
    peers += [partner] + [other_worker(j) for j in range(1, WORKERS)]
    for peer in peers:
        pl.semaphore_signal(barrier, inc=1, device_id=peer, device_id_type=MESH)

    cot_here = [local(c_ref, cb.at[o, tokens(exc[o])], L_COT + o) for o in range(2)]
    w_here = local(w_ref, wb.at[0, gat[0]], L_W)
    feat_here = [
        local(f_ref.at[:, column(o, g, exc[o])], fb.at[o, g, tokens(exc[o])], L_FEAT + o * RING + g)
        for o in range(2)
        for g in range(RING)
    ]
    ins = [
        local(src, dst, L_IN + i)
        for i, (src, dst) in enumerate(
            ((w_ref, wv), (fm_ref, fmv), (sm_ref, smv), (fa_ref, fav), (om_ref, omv),
             (fl_ref.at[pl.ds(pl.multiple_of(worker * PART, 8), PART)], fr.at[0]))
        )
    ]
    pl.semaphore_wait(barrier, len(peers))

    side = (1, RING - 1)
    cot1 = [
        [send(c_ref, cb.at[o, tokens(exc[o])], S_COT1 + 2 * o + i, along_exchange(o, side[i])) for i in range(2)]
        for o in range(2)
    ]
    wz = send(w_ref, wb.at[1, gat[0]], S_WZ, partner)
    loc = [
        send(
            fl_ref.at[pl.ds(pl.multiple_of((worker + j) % WORKERS * PART, 8), PART)],
            fr.at[j], S_LOC + j - 1, other_worker(j),
        )
        for j in range(1, WORKERS)
    ]
    feat = []
    for d in (2, 1, 3):
        for o in range(2):
            for g in range(RING):
                feat.append(
                    send(
                        f_ref.at[:, column(o, g, (exc[o] + d) % RING)],
                        fb.at[o, g, tokens(exc[o])],
                        S_FEAT + (o * 3 + d - 1) * RING + g,
                        along_exchange(o, d),
                    )
                )
    w1 = [[send(w_ref, wb.at[0, gat[0]], S_W1 + i, along_gather(0, side[i])) for i in range(2)], None]

    for copy in cot_here:
        copy.wait()
    cot2 = []
    for o in range(2):
        for i in range(2):
            cot1[o][i].wait_recv()
            block = (exc[o] + RING - side[i]) % RING
            rows = cb.at[o, tokens(block, i)]
            cot2.append(send(rows, rows, S_COT2 + 2 * o + i, along_exchange(o, side[i])))

    for copy in ins:
        copy.wait()
    total = jnp.zeros((PART, COLS), F32)
    anchor = fav[pl.ds(pl.multiple_of(worker * PART, 8), PART), :]
    for j in range(WORKERS):
        if j:
            loc[j - 1].wait_recv()
        total = total + (anchor - fr[j])
    mine = pl.ds(pl.multiple_of(worker * PART, 8), PART)
    ps[mine, :] = total
    pse = [send(ps.at[mine], ps.at[mine], S_PSE + j - 1, other_worker(j)) for j in range(1, WORKERS)]

    for copy in feat_here:
        copy.wait()
    for copy in feat + cot2:
        copy.wait_recv()

    def partial(o, g):
        gb[o, g] = lax.dot_general(
            fb[o, g], cb[o], (((0,), (0,)), ((), ())), preferred_element_type=F32
        )

    half = ROWS // 2
    r1 = [[], []]
    for o in range(2):
        far = (gat[o] + 2) % RING
        partial(o, far)
        for i in range(2):
            r1[o].append(
                send(gb.at[o, far, pl.ds(i * half, half)], rh.at[o, i], S_R1 + 2 * o + i, along_gather(o, side[i]))
            )

    wz.wait_recv()
    w1[1] = [
        send(wb.at[1, gat[1]], wb.at[1, gat[1]], S_W1 + 2 + i, along_gather(1, side[i])) for i in range(2)
    ]

    for o in range(2):
        for i in range(2):
            partial(o, (gat[o] + side[i]) % RING)
    w_here.wait()
    w2 = [[], []]
    r2 = [[], []]

    def forward_w(o):
        for i in range(2):
            w1[o][i].wait_recv()
            block = (gat[o] + RING - side[i]) % RING
            rows = wb.at[o, block, pl.ds(i * half, half)]
            w2[o].append(send(rows, rows, S_W2 + 2 * o + i, along_gather(o, side[i])))

    def pass_on(o):
        for i in range(2):
            r1[o][i].wait_recv()
            block = (gat[o] + side[i]) % RING
            gb[o, block, pl.ds(i * half, half), :] = gb[o, block, pl.ds(i * half, half), :] + rh[o, i]
            r2[o].append(send(gb.at[o, block], rf.at[o, i], S_R2 + 2 * o + i, along_gather(o, side[i])))

    forward_w(0)
    pass_on(0)
    pass_on(1)
    for o in range(2):
        partial(o, gat[o])
    forward_w(1)

    out = []
    out_here = []

    def product(o):
        for g in range(RING):
            w = wb[o, g]
            high = w.astype(BF16)
            low = (w - high.astype(F32)).astype(BF16)
            dims = (((1,), (1,)), ((), ()))
            c = cb[o]
            ob[o, g] = lax.dot_general(c, high, dims, preferred_element_type=F32) + lax.dot_general(
                c, low, dims, preferred_element_type=F32
            )
            there = fg_ref.at[:, column(o, g, exc[o])]
            for d in (2, 1, 3):
                out.append(
                    send(
                        ob.at[o, g, tokens((exc[o] + d) % RING)], there,
                        S_OUT + (o * 3 + d - 1) * RING + g, along_exchange(o, d),
                    )
                )
            out_here.append(local(ob.at[o, g, tokens(exc[o])], there, L_OUT + o * RING + g))

    for copy in w2[0]:
        copy.wait_recv()
    product(0)

    for copy in r2[1]:
        copy.wait_recv()
    gb[1, gat[1]] = gb[1, gat[1]] + rf[1, 0] + rf[1, 1]
    gz = send(gb.at[1, gat[1]], zr, S_GZ, partner)

    for copy in w2[1]:
        copy.wait_recv()
    product(1)

    for copy in pse:
        copy.wait_recv()
    pseudo = ps[...] / WORKERS
    momentum = outer_mass * omv[...] + pseudo
    nmv[...] = momentum
    nav[...] = fav[...] - outer_rate * (pseudo + outer_mass * momentum)
    results = [local(nmv, nm_ref, L_RES), local(nav, na_ref, L_RES + 1)]

    for copy in r2[0]:
        copy.wait_recv()
    plane = gb[0, gat[0]] + rf[0, 0] + rf[0, 1]
    gz.wait_recv()
    gradient = plane + zr[...]
    weight = wv[...]
    first_new = first_decay * fmv[...] + (1.0 - first_decay) * gradient
    second_new = second_decay * smv[...] + (1.0 - second_decay) * gradient * gradient
    first_hat = first_new / (1.0 - first_decay**adam_count)
    second_hat = second_new / (1.0 - second_decay**adam_count)
    nfv[...] = first_new
    nsv[...] = second_new
    nwv[...] = weight - inner_rate * (first_hat / (jnp.sqrt(second_hat) + adam_epsilon) + weight_decay * weight)
    results += [local(nfv, nf_ref, L_RES + 2), local(nsv, ns_ref, L_RES + 3), local(nwv, nw_ref, L_RES + 4)]

    for copy in out:
        copy.wait_recv()
    for copy in results + out_here:
        copy.wait()
    for copy in sent:
        copy.wait_send()


def on_device(
    features, value_cotangent, value_weight, first_moment, second_moment, fragment_local, fragment_anchor,
    outer_momentum,
):
    hbm = pl.BlockSpec(memory_space=pltpu.HBM)
    param = jax.ShapeDtypeStruct((ROWS, COLS), F32)
    vparam = pltpu.VMEM((ROWS, COLS), F32)
    got = pl.pallas_call(
        kernel,
        name="backward",
        out_shape=(jax.ShapeDtypeStruct(features.shape, F32),) + (param,) * 5,
        in_specs=[hbm] * 8,
        out_specs=(hbm,) * 6,
        scratch_shapes=[
            pltpu.VMEM((2, RING, RING * TOK, ROWS), BF16),
            pltpu.VMEM((2, RING * TOK, COLS), BF16),
            pltpu.VMEM((2, RING, ROWS, COLS), F32),
            pltpu.VMEM((2, RING, ROWS, COLS), F32),
            pltpu.VMEM((2, 2, ROWS // 2, COLS), F32),
            pltpu.VMEM((2, 2, ROWS, COLS), F32),
            vparam,
            pltpu.VMEM((2, RING, RING * TOK, ROWS), F32),
            vparam, vparam, vparam, vparam, vparam,
            pltpu.VMEM((WORKERS, PART, COLS), F32),
            vparam,
            vparam, vparam, vparam, vparam, vparam,
            pltpu.SemaphoreType.DMA((N_REMOTE,)),
            pltpu.SemaphoreType.DMA((N_REMOTE,)),
            pltpu.SemaphoreType.DMA((N_LOCAL,)),
        ],
        compiler_params=pltpu.CompilerParams(
            collective_id=0, has_side_effects=True, vmem_limit_bytes=56 * 2**20
        ),
    )(
        features, value_cotangent, value_weight[0], first_moment[0], second_moment[0], fragment_local[0],
        fragment_anchor, outer_momentum,
    )
    feature_grad, weight_new, first_new, second_new, new_anchor, new_momentum = got
    return feature_grad, weight_new[None], first_new[None], second_new[None], new_anchor, new_momentum


def solution(mesh):
    tokens = P(("worker", "fsdp"), None)
    groups = P("worker", "fsdp", None)
    whole = P("fsdp", None)
    return jax.shard_map(
        on_device,
        mesh=mesh,
        in_specs=(tokens, tokens, groups, groups, groups, groups, whole, whole),
        out_specs=(tokens, groups, groups, groups, whole, whole),
        check_vma=False,
    )
```

time: 993 us -> 133 us (0.13)
  waiting for transfers between devices: 939 us -> 0 us
  Pallas kernels: 0 us -> 122 us
  matrix products: 25.3 us -> 0 us
  between operations: 15.5 us -> 0.69 us
  local copies, waits for them, and re-layouts: 0.02 us -> 10.2 us
    reduce_scatter x1 -> x0, waiting for transfers between devices: 700 us -> none  [on_device(): lax.psum_scatter(lax.dot_general(features, value_cotangent, (((0,), (0,))...]
    all_gather x1 -> x0, waiting for transfers between devices: 150 us -> none  [on_device(): lax.all_gather(weight, 'fsdp', axis=0, tiled=True)]
    pallas_call x0 -> x1, Pallas kernels: none -> 122 us  [on_device(): pl.pallas_call(kernel, name='backward', out_shape=(jax.ShapeDtypeStruct(f...]
    psum x1 -> x0, waiting for transfers between devices: 88.5 us -> none  [on_device(): pseudo_sum = lax.psum(fragment_anchor - fragment_local[0], 'worker')]
    dot_general x2 -> x0, matrix products: 25.3 us -> none  [the longest x1 16.2 us: on_device(): jnp.dot(wide_cot, lax.all_gather(weight, 'fsdp', axis=0, tiled=True).T, p...]
    unnamed x4 -> x16, local copies, waits for them, and re-layouts: 0.02 us -> 10.2 us
  transfers between devices with their start and end apart: 3 -> 0, of which waited for: 3 -> 0; matrix products, arithmetic and copies ran while one was open for 3% -> 0% of each run, Pallas kernels for 0% -> 0%
where the time goes in v1:
time: 133 us; the launch traced here: 132 us
  Pallas kernels  122 us (92%)
  local copies, waits for them, and re-layouts  10.2 us (8%)
    pallas_call x1, Pallas kernels, on_device(): pl.pallas_call(kernel, name='backward', out_shape=(jax.ShapeDtypeStruct(f...  122 us
    unnamed x16, local copies, waits for them, and re-layouts  10.2 us

profile of v1, /device:TPU:32, one launch (start us, length us, event | category | flops | bytes accessed | tf_op | source)
XLA Modules:
  0.0 132.4 jit_solution(4135982589465800127)
XLA Ops:
  0.6 121.5 %backward.1 = (f32[192,8192]{1,0:T(8,128)}, f32[256,512]{1,0:T(8,128)}, f32[256,512]{1,0:T(8,128)}, f32[256,512]{1,0:T(8,128)}, f32[256,512]{1,0:T(8,128)}, /*index=5*/f32[256,512]{1,0:T(8,128)}) custom-call(bf16[192,8192]{1,0:T(8,128)(2,1)} %f_ref.1, bf16[192,512]{1,0:T(8,128)(2,1)} %c_ref.1, f32[256,512]{1,0:T(8,128)} %bitcast.7, f32[256,512]{1,0:T(8,128)} %bitcast.8, ...), custom_call_target="tpu_custom_call" | custom-call | tf_op jit(solution)/shard_map/backward/pallas_call | solution.py:315
  122.2 0.0 copy-start.4
  122.2 0.0 copy-start.3
  122.2 0.0 copy-start.2
  122.2 0.0 copy-start.1
  122.2 0.0 copy-start
  122.2 6.2 %copy.20 = f32[192,8192]{1,0:T(8,128)} copy(f32[192,8192]{1,0:T(8,128)} %get-tuple-element.24) | data formatting | bytes 12582912
  128.5 0.0 copy-done.4
  128.5 0.8 copy.21
  129.3 0.0 copy-done.3
  129.3 0.8 copy.22
  130.0 0.0 copy-done.2
  130.0 0.8 copy.23
  130.8 0.0 copy-done.1
  130.8 0.8 copy.24
  131.6 0.0 copy-done
  131.6 0.8 copy.25
Async XLA Ops:
  122.2 6.3 %copy-start.4 = (f32[256,512]{1,0:T(8,128)S(1)}, f32[256,512]{1,0:T(8,128)}, u32[]{:S(2)}) copy-start(f32[256,512]{1,0:T(8,128)} %get-tuple-element.13) | copy-start | bytes 1572868
  122.2 7.1 %copy-start.3 = (f32[256,512]{1,0:T(8,128)S(1)}, f32[256,512]{1,0:T(8,128)}, u32[]{:S(2)}) copy-start(f32[256,512]{1,0:T(8,128)} %get-tuple-element.14) | copy-start | bytes 1572868
  122.2 7.9 %copy-start.2 = (f32[256,512]{1,0:T(8,128)S(1)}, f32[256,512]{1,0:T(8,128)}, u32[]{:S(2)}) copy-start(f32[256,512]{1,0:T(8,128)} %get-tuple-element.15) | copy-start | bytes 1572868
  122.2 8.7 %copy-start.1 = (f32[256,512]{1,0:T(8,128)S(1)}, f32[256,512]{1,0:T(8,128)}, u32[]{:S(2)}) copy-start(f32[256,512]{1,0:T(8,128)} %get-tuple-element.28) | copy-start | bytes 1572868
  122.2 9.4 %copy-start = (f32[256,512]{1,0:T(8,128)S(1)}, f32[256,512]{1,0:T(8,128)}, u32[]{:S(2)}) copy-start(f32[256,512]{1,0:T(8,128)} %get-tuple-element.29) | copy-start | bytes 1572868

commit v2 on v1

v2 whole, which is shorter than its diff:
```python
import jax
import jax.numpy as jnp
from jax import lax
from jax.experimental import pallas as pl
from jax.experimental.pallas import tpu as pltpu
from jax.sharding import PartitionSpec as P

MESH = pl.DeviceIdType.MESH
F32 = jnp.float32
BF16 = jnp.bfloat16

first_decay = 0.9
second_decay = 0.95
inner_rate = 0.001
weight_decay = 0.1
adam_epsilon = 1e-08
adam_count = 10.0
outer_rate = 0.7
outer_mass = 0.9

RING = 4
TOK = 192
ROWS = 256
COLS = 512
WORKERS = 8
PART = ROWS // WORKERS

_count = 0


def _take(n):
    global _count
    base = _count
    _count += n
    return base


S_FEAT = _take(2 * 3 * RING)
S_COT1 = _take(8)
S_COT2 = _take(4)
S_WZ = _take(2)
S_W1 = _take(8)
S_W2 = _take(4)
S_R1 = _take(4)
S_R2 = _take(8)
S_GZ = _take(1)
S_OUT = _take(2 * 3 * RING)
S_LOC = _take(WORKERS - 1)
S_PSE = _take(WORKERS - 1)
N_REMOTE = _count

L_FEAT = 0
L_COT = 8
L_W = 10
L_IN = 11
L_OUT = 17
L_RES = 25
N_LOCAL = 30

STEPS = 30847.0
MARK = 16


def encode(t):
    largest = jnp.max(jnp.abs(t), axis=0, keepdims=True)
    unit = jnp.maximum(largest * 1.01, 1e-30).astype(BF16).astype(F32)
    q = t * (STEPS / unit)
    n = jnp.minimum(jnp.floor(jnp.abs(q) + 0.5), STEPS)
    e = jnp.floor(n * (1.0 / 128.0))
    size = (1.0 + (n - 128.0 * e) * (1.0 / 128.0)) * jnp.exp2(e - 120.0)
    return jnp.where(q < 0, -size, size).astype(BF16), unit


def store_code(ref, t):
    code, unit = encode(t)
    rows = t.shape[0]
    ref[pl.ds(0, rows), :] = code
    ref[pl.ds(rows, MARK), :] = jnp.broadcast_to(unit, (MARK, t.shape[1])).astype(BF16)


def load_code(ref):
    rows = ref.shape[0] - MARK
    unit = ref[pl.ds(rows, MARK), :].astype(F32)[0:1]
    return decode(ref[pl.ds(0, rows), :], unit)


def decode(code, unit):
    v = code.astype(F32)
    a = jnp.abs(v)
    e = jnp.floor(jnp.log(a) * 1.4426950408889634 + 0.0025)
    n = jnp.floor(a * jnp.exp2(7.0 - e) + 0.5) + (e * 128.0 + 119.0 * 128.0)
    n = n * (unit * (1.0 / STEPS))
    return jnp.where(v < 0, -n, n)


def kernel(
    f_ref, c_ref, w_ref, fm_ref, sm_ref, fl_ref, fa_ref, om_ref,
    code_ref, nw_ref, nf_ref, ns_ref, na_ref, nm_ref,
    fb, cb, wb, gb, rh, rf, zr, ob, high, low, wv, fmv, smv, fav, omv, fr, ps,
    nwv, nfv, nsv, nav, nmv,
    ssem, rsem, lsem,
):
    worker = lax.axis_index("worker")
    place = lax.axis_index("fsdp")
    x, y, zh = place // 8, (place // 2) % RING, place % 2

    zo = (zh, 1 - zh)
    gat = tuple(x * (1 - z) + y * z for z in zo)
    exc = tuple(y * (1 - z) + x * z for z in zo)

    def along_gather(o, d):
        z = zo[o]
        xx, yy = (x + d * (1 - z)) % RING, (y + d * z) % RING
        return (worker, (xx * RING + yy) * 2 + zh)

    def along_exchange(o, d):
        z = zo[o]
        xx, yy = (x + d * z) % RING, (y + d * (1 - z)) % RING
        return (worker, (xx * RING + yy) * 2 + zh)

    partner = (worker, place + 1 - 2 * zh)

    def other_worker(j):
        return ((worker + j) % WORKERS, place)

    def column(o, g, e):
        z = zo[o]
        start = g * (2048 - 1536 * z) + e * (512 + 1536 * z) + z * ROWS
        return pl.ds(pl.multiple_of(start, ROWS), ROWS)

    def slab(o, g, e):
        z = zo[o]
        return g * (8 - 6 * z) + e * (2 + 6 * z) + z

    def tokens(e, half=None):
        if half is None:
            return pl.ds(pl.multiple_of(e * TOK, 16), TOK)
        return pl.ds(pl.multiple_of(e * TOK + half * (TOK // 2), 16), TOK // 2)

    sent = []

    def send(src, dst, sem, device):
        copy = pltpu.make_async_remote_copy(
            src_ref=src, dst_ref=dst, send_sem=ssem.at[sem], recv_sem=rsem.at[sem],
            device_id=device, device_id_type=MESH,
        )
        copy.start()
        sent.append(copy)
        return copy

    def local(src, dst, sem):
        copy = pltpu.make_async_copy(src, dst, lsem.at[sem])
        copy.start()
        return copy

    barrier = pltpu.get_barrier_semaphore()
    peers = [along_gather(0, d) for d in (1, 2, 3)] + [along_exchange(0, d) for d in (1, 2, 3)]
    peers += [partner] + [other_worker(j) for j in range(1, WORKERS)]
    for peer in peers:
        pl.semaphore_signal(barrier, inc=1, device_id=peer, device_id_type=MESH)

    cot_here = [local(c_ref, cb.at[o, tokens(exc[o])], L_COT + o) for o in range(2)]
    w_here = local(w_ref, wv, L_W)
    feat_here = [
        local(f_ref.at[:, column(o, g, exc[o])], fb.at[o, g, tokens(exc[o])], L_FEAT + o * RING + g)
        for o in range(2)
        for g in range(RING)
    ]
    ins = [
        local(src, dst, L_IN + i)
        for i, (src, dst) in enumerate(
            ((fm_ref, fmv), (sm_ref, smv), (fa_ref, fav), (om_ref, omv),
             (fl_ref.at[pl.ds(pl.multiple_of(worker * PART, 8), PART)], fr.at[0]))
        )
    ]
    pl.semaphore_wait(barrier, len(peers))

    side = (1, RING - 1)
    half = ROWS // 2

    def halves(i):
        return (i, 1 - i)

    cot1 = {}
    for part in range(2):
        for o in range(2):
            for i in range(2):
                h = halves(i)[part]
                cot1[o, i, h] = send(
                    c_ref.at[pl.ds(h * (TOK // 2), TOK // 2)], cb.at[o, tokens(exc[o], h)],
                    S_COT1 + 4 * o + 2 * i + h, along_exchange(o, side[i]),
                )
    w_here.wait()
    for h in range(2):
        store_code(wb.at[0, gat[0], h], wv[pl.ds(h * half, half), :])
    wz = [send(wb.at[0, gat[0], h], wb.at[1, gat[0], h], S_WZ + h, partner) for h in range(2)]
    feat = []
    for d in (2, 1, 3):
        for o in range(2):
            for g in range(RING):
                feat.append(
                    send(
                        f_ref.at[:, column(o, g, (exc[o] + d) % RING)],
                        fb.at[o, g, tokens(exc[o])],
                        S_FEAT + (o * 3 + d - 1) * RING + g,
                        along_exchange(o, d),
                    )
                )

    for copy in cot_here:
        copy.wait()
    cot2 = []
    for o in range(2):
        for i in range(2):
            cot1[o, i, i].wait_recv()
            rows = cb.at[o, tokens((exc[o] + RING - side[i]) % RING, i)]
            cot2.append(send(rows, rows, S_COT2 + 2 * o + i, along_exchange(o, side[i])))
    loc = [
        send(
            fl_ref.at[pl.ds(pl.multiple_of((worker + j) % WORKERS * PART, 8), PART)],
            fr.at[j], S_LOC + j - 1, other_worker(j),
        )
        for j in range(1, WORKERS)
    ]

    def multiply(o, g):
        for h in range(2):
            w = load_code(wb.at[o, g, h])
            top = w.astype(BF16)
            high[pl.ds(h * half, half), :] = top
            low[pl.ds(h * half, half), :] = (w - top.astype(F32)).astype(BF16)
        dims = (((1,), (1,)), ((), ()))

        def step(e, carry):
            c = cb[o, tokens(e)]
            t = lax.dot_general(c, high[...], dims, preferred_element_type=F32) + lax.dot_general(
                c, low[...], dims, preferred_element_type=F32
            )
            store_code(ob.at[o, g, e], t)
            return carry

        lax.fori_loop(0, RING, step, 0)

    out = []
    out_here = []

    def give(o, g, at):
        there = code_ref.at[slab(o, g, exc[o])]
        for d in (2, 1, 3):
            out.append(
                send(
                    ob.at[o, g, (exc[o] + d) % RING], there,
                    S_OUT + (o * 3 + d - 1) * RING + at, along_exchange(o, d),
                )
            )
        out_here.append(local(ob.at[o, g, exc[o]], there, L_OUT + o * RING + at))

    def product(o, at):
        g = (gat[o] + at) % RING
        multiply(o, g)
        give(o, g, at)

    for copy in feat_here:
        copy.wait()
    for key in cot1:
        if key[1] != key[2]:
            cot1[key].wait_recv()
    for copy in cot2:
        copy.wait_recv()
    multiply(0, gat[0])
    for copy in feat:
        copy.wait_recv()

    def partial(o, g):
        gb[o, g] = lax.dot_general(
            fb[o, g], cb[o], (((0,), (0,)), ((), ())), preferred_element_type=F32
        )

    r1, r2 = {}, {}
    for o in range(2):
        far = (gat[o] + 2) % RING
        partial(o, far)
        for i in range(2):
            r1[o, i] = send(
                gb.at[o, far, pl.ds(i * half, half)], rh.at[o, i], S_R1 + 2 * o + i, along_gather(o, side[i])
            )

    def hand(o, i, h):
        block = (gat[o] + side[i]) % RING
        r2[o, i, h] = send(
            gb.at[o, block, pl.ds(h * half, half)], rf.at[o, i, pl.ds(h * half, half)],
            S_R2 + 4 * o + 2 * i + h, along_gather(o, side[i]),
        )

    for o in range(2):
        for i in range(2):
            partial(o, (gat[o] + side[i]) % RING)
            hand(o, i, 1 - i)
    for o in range(2):
        for i in range(2):
            r1[o, i].wait_recv()
            block = (gat[o] + side[i]) % RING
            rows = pl.ds(i * half, half)
            gb[o, block, rows, :] = gb[o, block, rows, :] + rh[o, i]
            hand(o, i, i)

    w1, w2 = {}, {}

    def weights(o):
        for part in range(2):
            for i in range(2):
                h = halves(i)[part]
                rows = wb.at[o, gat[o], h]
                w1[o, i, h] = send(rows, rows, S_W1 + 4 * o + 2 * i + h, along_gather(o, side[i]))

    def forward(o):
        for i in range(2):
            w1[o, i, i].wait_recv()
            rows = wb.at[o, (gat[o] + RING - side[i]) % RING, i]
            w2[o, i] = send(rows, rows, S_W2 + 2 * o + i, along_gather(o, side[i]))

    weights(0)
    for copy in wz:
        copy.wait_recv()
    weights(1)
    give(0, gat[0], 0)
    for o in range(2):
        partial(o, gat[o])

    for copy in ins:
        copy.wait()
    mine = pl.ds(pl.multiple_of(worker * PART, 8), PART)
    anchor = fav[mine, :]
    total = anchor - fr[0]
    for j in range(1, WORKERS):
        loc[j - 1].wait_recv()
        total = total + (anchor - fr[j])
    ps[mine, :] = total

    def plane(o):
        for i in range(2):
            for h in range(2):
                r2[o, i, h].wait_recv()
        return gb[o, gat[o]] + rf[o, 0] + rf[o, 1]

    forward(0)
    gb[1, gat[1]] = plane(1)
    gz = send(gb.at[1, gat[1]], zr, S_GZ, partner)
    forward(1)
    pse = [send(ps.at[mine], ps.at[mine], S_PSE + j - 1, other_worker(j)) for j in range(1, WORKERS)]

    product(1, 0)
    for i in range(2):
        for o in range(2):
            w1[o, 1 - i, i].wait_recv()
            product(o, side[i])
    gb[0, gat[0]] = plane(0)
    for o in range(2):
        for i in range(2):
            w2[o, i].wait_recv()
        product(o, 2)

    for copy in pse:
        copy.wait_recv()
    pseudo = ps[...] / WORKERS
    momentum = outer_mass * omv[...] + pseudo
    nmv[...] = momentum
    nav[...] = fav[...] - outer_rate * (pseudo + outer_mass * momentum)
    results = [local(nmv, nm_ref, L_RES), local(nav, na_ref, L_RES + 1)]

    gz.wait_recv()
    gradient = gb[0, gat[0]] + zr[...]
    weight = wv[...]
    first_new = first_decay * fmv[...] + (1.0 - first_decay) * gradient
    second_new = second_decay * smv[...] + (1.0 - second_decay) * gradient * gradient
    first_hat = first_new / (1.0 - first_decay**adam_count)
    second_hat = second_new / (1.0 - second_decay**adam_count)
    nfv[...] = first_new
    nsv[...] = second_new
    nwv[...] = weight - inner_rate * (first_hat / (jnp.sqrt(second_hat) + adam_epsilon) + weight_decay * weight)
    results += [local(nfv, nf_ref, L_RES + 2), local(nsv, ns_ref, L_RES + 3), local(nwv, nw_ref, L_RES + 4)]

    for copy in out:
        copy.wait_recv()
    for copy in results + out_here:
        copy.wait()
    for copy in sent:
        copy.wait_send()


GROUP = 4


def finish(code_ref, *refs):
    fg_ref = refs[5]
    code, wide, stage, sems = refs[11:]
    groups = code_ref.shape[0] // GROUP
    loads = [
        pltpu.make_async_copy(code_ref.at[pl.ds(i * GROUP, GROUP)], code.at[pl.ds(i * GROUP, GROUP)], sems.at[0, i])
        for i in range(groups)
    ]
    stores = [
        pltpu.make_async_copy(
            wide.at[:, pl.ds(i * GROUP * ROWS, GROUP * ROWS)],
            fg_ref.at[:, pl.ds(i * GROUP * ROWS, GROUP * ROWS)],
            sems.at[1, i],
        )
        for i in range(groups)
    ]
    into = [pltpu.make_async_copy(refs[k], stage.at[k], sems.at[0, groups + k]) for k in range(5)]
    outof = [pltpu.make_async_copy(stage.at[k], refs[6 + k], sems.at[1, groups + k]) for k in range(5)]
    for copy in loads + into:
        copy.start()
    for i in range(groups):
        loads[i].wait()
        for k in range(i * GROUP, (i + 1) * GROUP):
            wide[:, pl.ds(k * ROWS, ROWS)] = load_code(code.at[k])
        stores[i].start()
        if i == groups - 2:
            for load, store in zip(into, outof):
                load.wait()
                store.start()
    for copy in stores + outof:
        copy.wait()


def on_device(
    features, value_cotangent, value_weight, first_moment, second_moment, fragment_local, fragment_anchor,
    outer_momentum,
):
    hbm = pl.BlockSpec(memory_space=pltpu.HBM)
    slabs = features.shape[1] // ROWS
    param = jax.ShapeDtypeStruct((ROWS, COLS), F32)
    vparam = pltpu.VMEM((ROWS, COLS), F32)
    got = pl.pallas_call(
        kernel,
        name="backward",
        out_shape=(jax.ShapeDtypeStruct((slabs, TOK + MARK, ROWS), BF16),) + (param,) * 5,
        in_specs=[hbm] * 8,
        out_specs=(hbm,) * 6,
        scratch_shapes=[
            pltpu.VMEM((2, RING, RING * TOK, ROWS), BF16),
            pltpu.VMEM((2, RING * TOK, COLS), BF16),
            pltpu.VMEM((2, RING, 2, ROWS // 2 + MARK, COLS), BF16),
            pltpu.VMEM((2, RING, ROWS, COLS), F32),
            pltpu.VMEM((2, 2, ROWS // 2, COLS), F32),
            pltpu.VMEM((2, 2, ROWS, COLS), F32),
            vparam,
            pltpu.VMEM((2, RING, RING, TOK + MARK, ROWS), BF16),
            pltpu.VMEM((ROWS, COLS), BF16),
            pltpu.VMEM((ROWS, COLS), BF16),
            vparam, vparam, vparam, vparam, vparam,
            pltpu.VMEM((WORKERS, PART, COLS), F32),
            vparam,
            vparam, vparam, vparam, vparam, vparam,
            pltpu.SemaphoreType.DMA((N_REMOTE,)),
            pltpu.SemaphoreType.DMA((N_REMOTE,)),
            pltpu.SemaphoreType.DMA((N_LOCAL,)),
        ],
        compiler_params=pltpu.CompilerParams(
            collective_id=0, has_side_effects=True, vmem_limit_bytes=56 * 2**20
        ),
    )(
        features, value_cotangent, value_weight[0], first_moment[0], second_moment[0], fragment_local[0],
        fragment_anchor, outer_momentum,
    )
    feature_grad, weight_new, first_new, second_new, new_anchor, new_momentum = pl.pallas_call(
        finish,
        name="finish",
        out_shape=(jax.ShapeDtypeStruct(features.shape, F32),) + (param,) * 5,
        in_specs=[hbm] * 6,
        out_specs=(hbm,) * 6,
        scratch_shapes=[
            pltpu.VMEM((slabs, TOK + MARK, ROWS), BF16),
            pltpu.VMEM(features.shape, F32),
            pltpu.VMEM((5, ROWS, COLS), F32),
            pltpu.SemaphoreType.DMA((2, slabs // GROUP + 5)),
        ],
        compiler_params=pltpu.CompilerParams(vmem_limit_bytes=60 * 2**20),
    )(*got)
    return feature_grad, weight_new[None], first_new[None], second_new[None], new_anchor, new_momentum


def solution(mesh):
    tokens = P(("worker", "fsdp"), None)
    groups = P("worker", "fsdp", None)
    whole = P("fsdp", None)
    return jax.shard_map(
        on_device,
        mesh=mesh,
        in_specs=(tokens, tokens, groups, groups, groups, groups, whole, whole),
        out_specs=(tokens, groups, groups, groups, whole, whole),
        check_vma=False,
    )
```

time: 133 us -> 105 us (0.79)
  Pallas kernels: 122 us -> 103 us
  local copies, waits for them, and re-layouts: 10.2 us -> 0 us
    pallas_call x1 -> x2, Pallas kernels: 122 us -> 103 us  [the longest x1 95.9 us: on_device(): pl.pallas_call(kernel, name='backward', out_shape=(jax.ShapeDtypeStruct((...]
    unnamed x16 -> x0, local copies, waits for them, and re-layouts: 10.2 us -> none
where the time goes in v2:
time: 105 us; the launch traced here: 103 us
  Pallas kernels  103 us (98%)
    pallas_call x1, Pallas kernels, on_device(): pl.pallas_call(kernel, name='backward', out_shape=(jax.ShapeDtypeStruct((...  95.9 us
    pallas_call x1, Pallas kernels, on_device(): pl.pallas_call(finish, name='finish', out_shape=(jax.ShapeDtypeStruct(fea...  6.6 us

profile of v2, /device:TPU:32, one launch (start us, length us, event | category | flops | bytes accessed | tf_op | source)
XLA Modules:
  0.0 103.3 jit_solution(13900667092054416148)
XLA Ops:
  0.6 95.9 %backward.1 = (bf16[32,208,256]{2,1,0:T(8,128)(2,1)}, f32[256,512]{1,0:T(8,128)}, f32[256,512]{1,0:T(8,128)}, f32[256,512]{1,0:T(8,128)}, f32[256,512]{1,0:T(8,128)}, /*index=5*/f32[256,512]{1,0:T(8,128)}) custom-call(bf16[192,8192]{1,0:T(8,128)(2,1)} %f_ref.1, bf16[192,512]{1,0:T(8,128)(2,1)} %c_ref.1, f32[256,512]{1,0:T(8,128)} %bitcast.7, ...), custom_call_target="tpu_custom_call" | custom-call | tf_op jit(solution)/shard_map/backward/pallas_call | solution.py:435
  96.6 6.6 %finish.1 = (f32[192,8192]{1,0:T(8,128)}, f32[256,512]{1,0:T(8,128)}, f32[256,512]{1,0:T(8,128)}, f32[256,512]{1,0:T(8,128)}, f32[256,512]{1,0:T(8,128)}, /*index=5*/f32[256,512]{1,0:T(8,128)}) custom-call(bf16[32,208,256]{2,1,0:T(8,128)(2,1)} %get-tuple-element.18.code_ref, f32[256,512]{1,0:T(8,128)} %get-tuple-element.19.refs_0_, ...), custom_call_target="tpu_custom_call" | custom-call | tf_op jit(solution)/shard_map/finish/pallas_call | solution.py:467

commit v3 on v2

--- a/solution.py
+++ b/solution.py
@@ -43,7 +43,7 @@
 S_W2 = _take(4)
 S_R1 = _take(4)
 S_R2 = _take(8)
-S_GZ = _take(1)
+S_GZ = _take(2)
 S_OUT = _take(2 * 3 * RING)
 S_LOC = _take(WORKERS - 1)
 S_PSE = _take(WORKERS - 1)
@@ -78,6 +78,11 @@
     ref[pl.ds(rows, MARK), :] = jnp.broadcast_to(unit, (MARK, t.shape[1])).astype(BF16)
 
 
+def code_of(ref, t):
+    store_code(ref, t)
+    return ref
+
+
 def load_code(ref):
     rows = ref.shape[0] - MARK
     unit = ref[pl.ds(rows, MARK), :].astype(F32)[0:1]
@@ -96,7 +101,7 @@
 def kernel(
     f_ref, c_ref, w_ref, fm_ref, sm_ref, fl_ref, fa_ref, om_ref,
     code_ref, nw_ref, nf_ref, ns_ref, na_ref, nm_ref,
-    fb, cb, wb, gb, rh, rf, zr, ob, high, low, wv, fmv, smv, fav, omv, fr, ps,
+    fb, cb, wb, gb, r1s, rh, r2s, rf, gs, zr, ob, high, low, wv, fmv, smv, fav, omv, fr, ps,
     nwv, nfv, nsv, nav, nmv,
     ssem, rsem, lsem,
 ):
@@ -159,8 +164,8 @@
     for peer in peers:
         pl.semaphore_signal(barrier, inc=1, device_id=peer, device_id_type=MESH)
 
+    w_here = local(w_ref, wv, L_W)
     cot_here = [local(c_ref, cb.at[o, tokens(exc[o])], L_COT + o) for o in range(2)]
-    w_here = local(w_ref, wv, L_W)
     feat_here = [
         local(f_ref.at[:, column(o, g, exc[o])], fb.at[o, g, tokens(exc[o])], L_FEAT + o * RING + g)
         for o in range(2)
@@ -173,10 +178,13 @@
              (fl_ref.at[pl.ds(pl.multiple_of(worker * PART, 8), PART)], fr.at[0]))
         )
     ]
+    half = ROWS // 2
+    w_here.wait()
+    for h in range(2):
+        store_code(wb.at[0, gat[0], h], wv[pl.ds(h * half, half), :])
     pl.semaphore_wait(barrier, len(peers))
 
     side = (1, RING - 1)
-    half = ROWS // 2
 
     def halves(i):
         return (i, 1 - i)
@@ -190,21 +198,16 @@
                     c_ref.at[pl.ds(h * (TOK // 2), TOK // 2)], cb.at[o, tokens(exc[o], h)],
                     S_COT1 + 4 * o + 2 * i + h, along_exchange(o, side[i]),
                 )
-    w_here.wait()
-    for h in range(2):
-        store_code(wb.at[0, gat[0], h], wv[pl.ds(h * half, half), :])
     wz = [send(wb.at[0, gat[0], h], wb.at[1, gat[0], h], S_WZ + h, partner) for h in range(2)]
-    feat = []
-    for d in (2, 1, 3):
-        for o in range(2):
-            for g in range(RING):
-                feat.append(
-                    send(
-                        f_ref.at[:, column(o, g, (exc[o] + d) % RING)],
-                        fb.at[o, g, tokens(exc[o])],
-                        S_FEAT + (o * 3 + d - 1) * RING + g,
-                        along_exchange(o, d),
-                    )
+    feat = {}
+    for at in (2, 1, 3, 0):
+        for d in (2, 1, 3):
+            for o in range(2):
+                feat[o, at, d] = send(
+                    f_ref.at[:, column(o, (gat[o] + at) % RING, (exc[o] + d) % RING)],
+                    fb.at[o, (gat[o] + at) % RING, tokens(exc[o])],
+                    S_FEAT + (o * 3 + d - 1) * RING + at,
+                    along_exchange(o, d),
                 )
 
     for copy in cot_here:
@@ -268,10 +271,11 @@
     for copy in cot2:
         copy.wait_recv()
     multiply(0, gat[0])
-    for copy in feat:
-        copy.wait_recv()
-
-    def partial(o, g):
+
+    def partial(o, at):
+        g = (gat[o] + at) % RING
+        for d in (2, 1, 3):
+            feat[o, at, d].wait_recv()
         gb[o, g] = lax.dot_general(
             fb[o, g], cb[o], (((0,), (0,)), ((), ())), preferred_element_type=F32
         )
@@ -279,29 +283,30 @@
     r1, r2 = {}, {}
     for o in range(2):
         far = (gat[o] + 2) % RING
-        partial(o, far)
+        partial(o, 2)
         for i in range(2):
             r1[o, i] = send(
-                gb.at[o, far, pl.ds(i * half, half)], rh.at[o, i], S_R1 + 2 * o + i, along_gather(o, side[i])
+                code_of(r1s.at[o, i], gb[o, far, pl.ds(i * half, half), :]), rh.at[o, i],
+                S_R1 + 2 * o + i, along_gather(o, side[i]),
             )
 
     def hand(o, i, h):
         block = (gat[o] + side[i]) % RING
         r2[o, i, h] = send(
-            gb.at[o, block, pl.ds(h * half, half)], rf.at[o, i, pl.ds(h * half, half)],
+            code_of(r2s.at[o, i, h], gb[o, block, pl.ds(h * half, half), :]), rf.at[o, i, h],
             S_R2 + 4 * o + 2 * i + h, along_gather(o, side[i]),
         )
 
-    for o in range(2):
-        for i in range(2):
-            partial(o, (gat[o] + side[i]) % RING)
+    for i in range(2):
+        for o in range(2):
+            partial(o, side[i])
             hand(o, i, 1 - i)
     for o in range(2):
         for i in range(2):
             r1[o, i].wait_recv()
             block = (gat[o] + side[i]) % RING
             rows = pl.ds(i * half, half)
-            gb[o, block, rows, :] = gb[o, block, rows, :] + rh[o, i]
+            gb[o, block, rows, :] = gb[o, block, rows, :] + load_code(rh.at[o, i])
             hand(o, i, i)
 
     w1, w2 = {}, {}
@@ -323,9 +328,8 @@
     for copy in wz:
         copy.wait_recv()
     weights(1)
-    give(0, gat[0], 0)
-    for o in range(2):
-        partial(o, gat[o])
+    for o in (1, 0):
+        partial(o, 0)
 
     for copy in ins:
         copy.wait()
@@ -336,25 +340,31 @@
         loc[j - 1].wait_recv()
         total = total + (anchor - fr[j])
     ps[mine, :] = total
+    pse = [send(ps.at[mine], ps.at[mine], S_PSE + j - 1, other_worker(j)) for j in range(1, WORKERS)]
 
     def plane(o):
         for i in range(2):
             for h in range(2):
                 r2[o, i, h].wait_recv()
-        return gb[o, gat[o]] + rf[o, 0] + rf[o, 1]
-
+        for h in range(2):
+            rows = pl.ds(h * half, half)
+            gb[o, gat[o], rows, :] = gb[o, gat[o], rows, :] + load_code(rf.at[o, 0, h]) + load_code(rf.at[o, 1, h])
+
+    plane(1)
+    gz = [
+        send(code_of(gs.at[h], gb[1, gat[1], pl.ds(h * half, half), :]), zr.at[h], S_GZ + h, partner)
+        for h in range(2)
+    ]
     forward(0)
-    gb[1, gat[1]] = plane(1)
-    gz = send(gb.at[1, gat[1]], zr, S_GZ, partner)
     forward(1)
-    pse = [send(ps.at[mine], ps.at[mine], S_PSE + j - 1, other_worker(j)) for j in range(1, WORKERS)]
+    give(0, gat[0], 0)
 
     product(1, 0)
     for i in range(2):
         for o in range(2):
             w1[o, 1 - i, i].wait_recv()
             product(o, side[i])
-    gb[0, gat[0]] = plane(0)
+    plane(0)
     for o in range(2):
         for i in range(2):
             w2[o, i].wait_recv()
@@ -368,16 +378,20 @@
     nav[...] = fav[...] - outer_rate * (pseudo + outer_mass * momentum)
     results = [local(nmv, nm_ref, L_RES), local(nav, na_ref, L_RES + 1)]
 
-    gz.wait_recv()
-    gradient = gb[0, gat[0]] + zr[...]
-    weight = wv[...]
-    first_new = first_decay * fmv[...] + (1.0 - first_decay) * gradient
-    second_new = second_decay * smv[...] + (1.0 - second_decay) * gradient * gradient
-    first_hat = first_new / (1.0 - first_decay**adam_count)
-    second_hat = second_new / (1.0 - second_decay**adam_count)
-    nfv[...] = first_new
-    nsv[...] = second_new
-    nwv[...] = weight - inner_rate * (first_hat / (jnp.sqrt(second_hat) + adam_epsilon) + weight_decay * weight)
+    for h in range(2):
+        gz[h].wait_recv()
+        rows = pl.ds(h * half, half)
+        gradient = gb[0, gat[0], rows, :] + load_code(zr.at[h])
+        weight = wv[rows, :]
+        first_new = first_decay * fmv[rows, :] + (1.0 - first_decay) * gradient
+        second_new = second_decay * smv[rows, :] + (1.0 - second_decay) * gradient * gradient
+        first_hat = first_new / (1.0 - first_decay**adam_count)
+        second_hat = second_new / (1.0 - second_decay**adam_count)
+        nfv[rows, :] = first_new
+        nsv[rows, :] = second_new
+        nwv[rows, :] = weight - inner_rate * (
+            first_hat / (jnp.sqrt(second_hat) + adam_epsilon) + weight_decay * weight
+        )
     results += [local(nfv, nf_ref, L_RES + 2), local(nsv, ns_ref, L_RES + 3), local(nwv, nw_ref, L_RES + 4)]
 
     for copy in out:
@@ -443,9 +457,12 @@
             pltpu.VMEM((2, RING * TOK, COLS), BF16),
             pltpu.VMEM((2, RING, 2, ROWS // 2 + MARK, COLS), BF16),
             pltpu.VMEM((2, RING, ROWS, COLS), F32),
-            pltpu.VMEM((2, 2, ROWS // 2, COLS), F32),
-            pltpu.VMEM((2, 2, ROWS, COLS), F32),
-            vparam,
+            pltpu.VMEM((2, 2, ROWS // 2 + MARK, COLS), BF16),
+            pltpu.VMEM((2, 2, ROWS // 2 + MARK, COLS), BF16),
+            pltpu.VMEM((2, 2, 2, ROWS // 2 + MARK, COLS), BF16),
+            pltpu.VMEM((2, 2, 2, ROWS // 2 + MARK, COLS), BF16),
+            pltpu.VMEM((2, ROWS // 2 + MARK, COLS), BF16),
+            pltpu.VMEM((2, ROWS // 2 + MARK, COLS), BF16),
             pltpu.VMEM((2, RING, RING, TOK + MARK, ROWS), BF16),
             pltpu.VMEM((ROWS, COLS), BF16),
             pltpu.VMEM((ROWS, COLS), BF16),

time: 105 us -> 86.6 us (0.82); the launches traced: 103 us -> 86.5 us
  Pallas kernels: 103 us -> 85.7 us
    pallas_call x1, Pallas kernels: 95.9 us -> 79.1 us  [on_device(): pl.pallas_call(kernel, name='backward', out_shape=(jax.ShapeDtypeStruct((...]
where the time goes in v3:
time: 86.6 us; the launch traced here: 86.5 us
  Pallas kernels  85.7 us (99%)
    pallas_call x1, Pallas kernels, on_device(): pl.pallas_call(kernel, name='backward', out_shape=(jax.ShapeDtypeStruct((...  79.1 us
    pallas_call x1, Pallas kernels, on_device(): pl.pallas_call(finish, name='finish', out_shape=(jax.ShapeDtypeStruct(fea...  6.6 us

profile of v3, /device:TPU:32, one launch (start us, length us, event | category | flops | bytes accessed | tf_op | source)
XLA Modules:
  0.0 86.5 jit_solution(5533748639603290116)
XLA Ops:
  0.6 79.1 %backward.1 = (bf16[32,208,256]{2,1,0:T(8,128)(2,1)}, f32[256,512]{1,0:T(8,128)}, f32[256,512]{1,0:T(8,128)}, f32[256,512]{1,0:T(8,128)}, f32[256,512]{1,0:T(8,128)}, /*index=5*/f32[256,512]{1,0:T(8,128)}) custom-call(bf16[192,8192]{1,0:T(8,128)(2,1)} %f_ref.1, bf16[192,512]{1,0:T(8,128)(2,1)} %c_ref.1, f32[256,512]{1,0:T(8,128)} %bitcast.7, ...), custom_call_target="tpu_custom_call" | custom-call | tf_op jit(solution)/shard_map/backward/pallas_call | solution.py:449
  79.8 6.6 %finish.1 = (f32[192,8192]{1,0:T(8,128)}, f32[256,512]{1,0:T(8,128)}, f32[256,512]{1,0:T(8,128)}, f32[256,512]{1,0:T(8,128)}, f32[256,512]{1,0:T(8,128)}, /*index=5*/f32[256,512]{1,0:T(8,128)}) custom-call(bf16[32,208,256]{2,1,0:T(8,128)(2,1)} %get-tuple-element.18.code_ref, f32[256,512]{1,0:T(8,128)} %get-tuple-element.19.refs_0_, ...), custom_call_target="tpu_custom_call" | custom-call | tf_op jit(solution)/shard_map/finish/pallas_call | solution.py:484

commit v4 on v3

--- a/solution.py
+++ b/solution.py
@@ -58,7 +58,7 @@
 N_LOCAL = 30
 
 STEPS = 30847.0
-MARK = 16
+MARK = 8
 
 
 def encode(t):
@@ -200,7 +200,8 @@
                 )
     wz = [send(wb.at[0, gat[0], h], wb.at[1, gat[0], h], S_WZ + h, partner) for h in range(2)]
     feat = {}
-    for at in (2, 1, 3, 0):
+
+    def features(at):
         for d in (2, 1, 3):
             for o in range(2):
                 feat[o, at, d] = send(
@@ -210,6 +211,8 @@
                     along_exchange(o, d),
                 )
 
+    features(2)
+
     for copy in cot_here:
         copy.wait()
     cot2 = []
@@ -218,6 +221,8 @@
             cot1[o, i, i].wait_recv()
             rows = cb.at[o, tokens((exc[o] + RING - side[i]) % RING, i)]
             cot2.append(send(rows, rows, S_COT2 + 2 * o + i, along_exchange(o, side[i])))
+    for at in (1, 3, 0):
+        features(at)
     loc = [
         send(
             fl_ref.at[pl.ds(pl.multiple_of((worker + j) % WORKERS * PART, 8), PART)],

time: 86.6 us -> 80.4 us (0.928)
  Pallas kernels: 85.7 us -> 79.5 us
    pallas_call x1, Pallas kernels: 79.1 us -> 72.9 us  [on_device(): pl.pallas_call(kernel, name='backward', out_shape=(jax.ShapeDtypeStruct((...]
where the time goes in v4:
time: 80.4 us; the launch traced here: 80.3 us
  Pallas kernels  79.5 us (99%)
    pallas_call x1, Pallas kernels, on_device(): pl.pallas_call(kernel, name='backward', out_shape=(jax.ShapeDtypeStruct((...  72.9 us
    pallas_call x1, Pallas kernels, on_device(): pl.pallas_call(finish, name='finish', out_shape=(jax.ShapeDtypeStruct(fea...  6.6 us

profile of v4, /device:TPU:32, one launch (start us, length us, event | category | flops | bytes accessed | tf_op | source)
XLA Modules:
  0.0 80.3 jit_solution(16896926382830795616)
XLA Ops:
  0.6 72.9 %backward.1 = (bf16[32,200,256]{2,1,0:T(8,128)(2,1)}, f32[256,512]{1,0:T(8,128)}, f32[256,512]{1,0:T(8,128)}, f32[256,512]{1,0:T(8,128)}, f32[256,512]{1,0:T(8,128)}, /*index=5*/f32[256,512]{1,0:T(8,128)}) custom-call(bf16[192,8192]{1,0:T(8,128)(2,1)} %f_ref.1, bf16[192,512]{1,0:T(8,128)(2,1)} %c_ref.1, f32[256,512]{1,0:T(8,128)} %bitcast.7, ...), custom_call_target="tpu_custom_call" | custom-call | tf_op jit(solution)/shard_map/backward/pallas_call | solution.py:454
  73.6 6.6 %finish.1 = (f32[192,8192]{1,0:T(8,128)}, f32[256,512]{1,0:T(8,128)}, f32[256,512]{1,0:T(8,128)}, f32[256,512]{1,0:T(8,128)}, f32[256,512]{1,0:T(8,128)}, /*index=5*/f32[256,512]{1,0:T(8,128)}) custom-call(bf16[32,200,256]{2,1,0:T(8,128)(2,1)} %get-tuple-element.18.code_ref, f32[256,512]{1,0:T(8,128)} %get-tuple-element.19.refs_0_, ...), custom_call_target="tpu_custom_call" | custom-call | tf_op jit(solution)/shard_map/finish/pallas_call | solution.py:489

commit v5 on v4

--- a/solution.py
+++ b/solution.py
@@ -93,9 +93,9 @@
     v = code.astype(F32)
     a = jnp.abs(v)
     e = jnp.floor(jnp.log(a) * 1.4426950408889634 + 0.0025)
-    n = jnp.floor(a * jnp.exp2(7.0 - e) + 0.5) + (e * 128.0 + 119.0 * 128.0)
-    n = n * (unit * (1.0 / STEPS))
-    return jnp.where(v < 0, -n, n)
+    n = a * jnp.exp2(7.0 - e) + (e * 128.0 + 119.0 * 128.0)
+    step = unit * (1.0 / STEPS)
+    return n * jnp.where(v < 0, -step, step)
 
 
 def kernel(

time: 80.4 us -> 79.5 us (0.989)
  Pallas kernels: 79.5 us -> 78.6 us
where the time goes in v5:
time: 79.5 us; the launch traced here: 79.4 us
  Pallas kernels  78.6 us (99%)
  between operations  0.8 us (1%)
    pallas_call x1, Pallas kernels, on_device(): pl.pallas_call(kernel, name='backward', out_shape=(jax.ShapeDtypeStruct((...  72.5 us
    pallas_call x1, Pallas kernels, on_device(): pl.pallas_call(finish, name='finish', out_shape=(jax.ShapeDtypeStruct(fea...  6.11 us

profile of v5, /device:TPU:32, one launch (start us, length us, event | category | flops | bytes accessed | tf_op | source)
XLA Modules:
  0.0 79.4 jit_solution(9527321555917037171)
XLA Ops:
  0.6 72.5 %backward.1 = (bf16[32,200,256]{2,1,0:T(8,128)(2,1)}, f32[256,512]{1,0:T(8,128)}, f32[256,512]{1,0:T(8,128)}, f32[256,512]{1,0:T(8,128)}, f32[256,512]{1,0:T(8,128)}, /*index=5*/f32[256,512]{1,0:T(8,128)}) custom-call(bf16[192,8192]{1,0:T(8,128)(2,1)} %f_ref.1, bf16[192,512]{1,0:T(8,128)(2,1)} %c_ref.1, f32[256,512]{1,0:T(8,128)} %bitcast.7, ...), custom_call_target="tpu_custom_call" | custom-call | tf_op jit(solution)/shard_map/backward/pallas_call | solution.py:454
  73.1 6.1 %finish.1 = (f32[192,8192]{1,0:T(8,128)}, f32[256,512]{1,0:T(8,128)}, f32[256,512]{1,0:T(8,128)}, f32[256,512]{1,0:T(8,128)}, f32[256,512]{1,0:T(8,128)}, /*index=5*/f32[256,512]{1,0:T(8,128)}) custom-call(bf16[32,200,256]{2,1,0:T(8,128)(2,1)} %get-tuple-element.18.code_ref, f32[256,512]{1,0:T(8,128)} %get-tuple-element.19.refs_0_, ...), custom_call_target="tpu_custom_call" | custom-call | tf_op jit(solution)/shard_map/finish/pallas_call | solution.py:489

commit v6 on v5

--- a/solution.py
+++ b/solution.py
@@ -435,7 +435,7 @@
         for k in range(i * GROUP, (i + 1) * GROUP):
             wide[:, pl.ds(k * ROWS, ROWS)] = load_code(code.at[k])
         stores[i].start()
-        if i == groups - 2:
+        if i == groups - 1:
             for load, store in zip(into, outof):
                 load.wait()
                 store.start()

time: 79.5 us -> 79.7 us (level)
  no operation moved by 1% of the time
where the time goes in v6:
time: 79.7 us; the launch traced here: 79.6 us
  Pallas kernels  78.8 us (99%)
  between operations  0.8 us (1%)
    pallas_call x1, Pallas kernels, on_device(): pl.pallas_call(kernel, name='backward', out_shape=(jax.ShapeDtypeStruct((...  72.5 us
    pallas_call x1, Pallas kernels, on_device(): pl.pallas_call(finish, name='finish', out_shape=(jax.ShapeDtypeStruct(fea...  6.29 us

profile of v6, /device:TPU:32, one launch (start us, length us, event | category | flops | bytes accessed | tf_op | source)
XLA Modules:
  0.0 79.6 jit_solution(6193899090135813849)
XLA Ops:
  0.6 72.5 %backward.1 = (bf16[32,200,256]{2,1,0:T(8,128)(2,1)}, f32[256,512]{1,0:T(8,128)}, f32[256,512]{1,0:T(8,128)}, f32[256,512]{1,0:T(8,128)}, f32[256,512]{1,0:T(8,128)}, /*index=5*/f32[256,512]{1,0:T(8,128)}) custom-call(bf16[192,8192]{1,0:T(8,128)(2,1)} %f_ref.1, bf16[192,512]{1,0:T(8,128)(2,1)} %c_ref.1, f32[256,512]{1,0:T(8,128)} %bitcast.7, ...), custom_call_target="tpu_custom_call" | custom-call | tf_op jit(solution)/shard_map/backward/pallas_call | solution.py:454
  73.1 6.3 %finish.1 = (f32[192,8192]{1,0:T(8,128)}, f32[256,512]{1,0:T(8,128)}, f32[256,512]{1,0:T(8,128)}, f32[256,512]{1,0:T(8,128)}, f32[256,512]{1,0:T(8,128)}, /*index=5*/f32[256,512]{1,0:T(8,128)}) custom-call(bf16[32,200,256]{2,1,0:T(8,128)(2,1)} %get-tuple-element.18.code_ref, f32[256,512]{1,0:T(8,128)} %get-tuple-element.19.refs_0_, ...), custom_call_target="tpu_custom_call" | custom-call | tf_op jit(solution)/shard_map/finish/pallas_call | solution.py:489
